TPU v7x, 128 devices: a whole 4x4x4 slice. The times are simulated.
128 devices in a mesh: pool: 16 (over y, x), tensor: 8 (over z, core).
Axes of the slice: x: 4, y: 4, z: 4, core: 2. Of those that a mesh axis runs over, the one named last changes fastest.
Arguments:
- inputs: bfloat16 [1024, 8192], P(None, 'pool'), may hold values from -160 to 160
- attn_gain: bfloat16 [8192], P('pool'), may hold values from 0.5 to 1.5
- query_key_value_weight: bfloat16 [8192, 10240], P('pool', 'tensor'), may hold values from -0.0625 to 0.0625
- key_value_pages: bfloat16 [1024, 128, 8, 256], P('pool', None, 'tensor'), may hold values from -210 to 210, as said below
- w_out: bfloat16 [8192, 8192], P('tensor', 'pool'), may hold values from -0.5 to 0.5
- ffn_gain: bfloat16 [8192], P('pool'), may hold values from 0.5 to 1.5
- w_gate_up: bfloat16 [8192, 2, 28672], P('pool', None, 'tensor'), may hold values from -0.0625 to 0.0625
- w_down: bfloat16 [28672, 8192], P('tensor', 'pool'), may hold values from -0.0625 to 0.0625
- owner_pool_device: int32 [1024], replicated, may hold values from 0 to 15, as said below
- context_page_count: int32 [1024], replicated, may hold values from 1 to 8, as said below
- request_page_slots: int32 [1024, 8], replicated, may hold values from 0 to 63
- mig_page: int32 [16, 16], P('pool'), may hold values from 0 to 63
- mig_dest: int32 [16, 16], P('pool'), may hold values from 0 to 15, as said below
- mig_slot: int32 [16, 16], P('pool'), may hold values from 0 to 63, as said below
Outputs:
- out_rows: bfloat16 [1024, 8192], P(None, 'pool')
- new_pool: bfloat16 [1024, 128, 8, 256], P('pool', None, 'tensor')
Inputs may be any that keep to these rules, and one draw needn't show every extreme that they name: `key_value_pages`: cached keys (first 128 entries of the last dimension, rotary embedding already applied) and values (last 128). `owner_pool_device`: each aligned block of 64 requests names every pool device at most 8 times, and in every block one pool device is named exactly 8 times. `context_page_count`: at least one request has exactly 8 pages. `request_page_slots`: entries at or beyond a request's page count are not used. `mig_dest`: no row names one destination more than 2 times, and every row names one exactly 2 times. `mig_slot`: no two moved pages take the same slot of the same destination.
All inputs are finite; a program needn't handle non-finite values.
Results may differ from a plain program's by a relative error of at most 0.013.
Values may be sent and summed in bfloat16 or wider, within the bound.
No kernel may reach another device: no remote copies, remote signals or barrier semaphores. Data moves between devices by JAX's collectives and lax.ppermute only.
A program may use at most 192 MiB of HBM per device.

v0:
```python
import math
import jax
import jax.numpy as jnp
from jax import lax
from jax.sharding import PartitionSpec as P

MCAP = 2
epsilon = 1e-05


def rotate_halves(vectors, token_positions):
    half_dim = vectors.shape[-1] // 2
    steps_index = jnp.arange(half_dim, dtype=jnp.float32)
    frequency = jnp.exp(steps_index * (-2.0 * math.log(500000.0) / vectors.shape[-1]))
    angles = token_positions.astype(jnp.float32)[:, None] * frequency[None, :]
    cosine = jnp.cos(angles)[:, None, :]
    sine_part = jnp.sin(angles)[:, None, :]
    front_half = vectors[..., :half_dim]
    back_half = vectors[..., half_dim:]
    return jnp.concatenate(
        [front_half * cosine - back_half * sine_part, back_half * cosine + front_half * sine_part],
        axis=-1,
    )


def per_device(
    inputs,
    attn_gain,
    query_key_value_weight,
    key_value_pages,
    w_out,
    ffn_gain,
    w_gate_up,
    w_down,
    owner_pool_device,
    context_page_count,
    request_page_slots,
    mig_page,
    mig_dest,
    mig_slot,
):
    pool_count = lax.axis_size("pool")
    pool_here = lax.axis_index("pool")
    total_req = inputs.shape[0]
    per_block = total_req // pool_count
    local_width = inputs.shape[1]
    full_width = local_width * pool_count
    page_len = key_value_pages.shape[1]
    kv_local = key_value_pages.shape[2]
    head_dim = key_value_pages.shape[3] // 2
    query_groups = query_key_value_weight.shape[1] // (kv_local * head_dim) - 2
    capacity = max(2, (2 * per_block + pool_count - 1) // pool_count)
    scale = 1.0 / math.sqrt(head_dim)
    residual = inputs.astype(jnp.float32)
    squares = lax.psum(jnp.sum(residual * residual, axis=1), "pool")
    normed_input = (
        residual
        * lax.rsqrt(squares[:, None] / full_width + epsilon)
        * attn_gain.astype(jnp.float32)
    ).astype(jnp.bfloat16)
    block_owner = owner_pool_device.reshape(pool_count, per_block)
    pool_iota = jnp.arange(pool_count, dtype=jnp.int32)
    owner_hot = (block_owner[:, :, None] == pool_iota[None, None, :]).astype(jnp.int32)
    slot_rank = jnp.sum(jnp.cumsum(owner_hot, axis=1) * owner_hot, axis=2) - 1
    slot_iota = jnp.arange(capacity, dtype=jnp.int32)
    own_rows = lax.psum_scatter(
        jnp.dot(normed_input, query_key_value_weight, preferred_element_type=jnp.float32),
        "pool",
        scatter_dimension=0,
        tiled=True,
    )
    my_lengths = lax.dynamic_slice_in_dim(context_page_count, pool_here * per_block, per_block)
    token_positions = my_lengths * page_len
    item_count = own_rows.shape[0]
    parts = own_rows.reshape(item_count, kv_local, query_groups + 2, head_dim)
    query = rotate_halves(
        parts[:, :, :query_groups].reshape(item_count, kv_local * query_groups, head_dim),
        token_positions,
    ).reshape(item_count, kv_local, query_groups, head_dim)
    own_key = rotate_halves(parts[:, :, query_groups], token_positions)[:, :, None, :]
    own_val = parts[:, :, query_groups + 1][:, :, None, :]
    ready_rows = (
        jnp.concatenate([query, own_key, own_val], axis=2)
        .astype(jnp.bfloat16)
        .reshape(item_count, -1)
    )
    my_owner = block_owner[pool_here]
    my_rank = slot_rank[pool_here]
    slot_hits = (my_owner[:, None, None] == pool_iota[None, :, None]) & (
        my_rank[:, None, None] == slot_iota[None, None, :]
    )
    local_iota = jnp.arange(per_block, dtype=jnp.int32)
    local_pick = jnp.sum(jnp.where(slot_hits, local_iota[:, None, None], 0), axis=0)
    filled = jnp.any(slot_hits, axis=0)
    send_rows = jnp.where(
        filled[:, :, None], jnp.take(ready_rows, local_pick, axis=0), jnp.zeros((), jnp.bfloat16)
    )
    send_ids = jnp.where(filled, pool_here * per_block + local_pick, total_req)
    rows_all = lax.all_to_all(send_rows, "pool", split_axis=0, concat_axis=0, tiled=True)
    ids_all = lax.all_to_all(send_ids, "pool", split_axis=0, concat_axis=0, tiled=True)

    def one_block(blocks):
        rows_b, ids_b = blocks
        item_count = ids_b.shape[0]
        safe_ids = jnp.minimum(ids_b, total_req - 1)
        lengths = context_page_count[safe_ids]
        table = request_page_slots[safe_ids]
        context_span = table.shape[1] * page_len
        gathered_pages = key_value_pages[table].reshape(
            item_count, context_span, kv_local, 2 * head_dim
        )
        keys = gathered_pages[..., :head_dim]
        values = gathered_pages[..., head_dim:]
        parts = rows_b.reshape(item_count, kv_local, query_groups + 2, head_dim)
        query = parts[:, :, :query_groups]
        own_key = parts[:, :, query_groups]
        own_val = parts[:, :, query_groups + 1]
        scores = (
            jnp.einsum("nhgd,nthd->nhgt", query, keys, preferred_element_type=jnp.float32) * scale
        )
        valid = (jnp.arange(context_span)[None, :] < (lengths * page_len)[:, None])[
            :, None, None, :
        ]
        scores = jnp.where(valid, scores, -1e30)
        self_score = (
            jnp.einsum("nhgd,nhd->nhg", query, own_key, preferred_element_type=jnp.float32) * scale
        )
        top = jnp.maximum(jnp.max(scores, axis=-1), self_score)
        expo = jnp.where(valid, jnp.exp(scores - top[..., None]), 0.0)
        self_exp = jnp.exp(self_score - top)
        total = jnp.sum(expo, axis=-1) + self_exp
        weights = (expo / total[..., None]).astype(jnp.bfloat16)
        self_weight = (self_exp / total).astype(jnp.bfloat16)
        mixed = jnp.einsum("nhgt,nthd->nhgd", weights, values, preferred_element_type=jnp.float32)
        mixed = (
            mixed
            + self_weight.astype(jnp.float32)[..., None]
            * own_val.astype(jnp.float32)[:, :, None, :]
        )
        return mixed.astype(jnp.bfloat16).reshape(item_count, -1)

    attn_buf = lax.map(one_block, (rows_all, ids_all))
    returned = lax.all_to_all(attn_buf, "pool", split_axis=0, concat_axis=0, tiled=True)
    my_rows = returned[block_owner[pool_here], slot_rank[pool_here]]
    partial_value = jnp.dot(
        lax.all_gather(my_rows, "pool", axis=0, tiled=True),
        w_out,
        preferred_element_type=jnp.float32,
    )
    middle = residual + lax.psum(partial_value, "tensor")
    mid_squares = lax.psum(jnp.sum(middle * middle, axis=1), "pool")
    ffn_in = (
        middle
        * lax.rsqrt(mid_squares[:, None] / full_width + epsilon)
        * ffn_gain.astype(jnp.float32)
    ).astype(jnp.bfloat16)
    hidden_local = w_gate_up.shape[2]
    joined_weight = w_gate_up.reshape(local_width, 2 * hidden_local)
    gate_up = lax.psum_scatter(
        jnp.dot(ffn_in, joined_weight, preferred_element_type=jnp.float32),
        "pool",
        scatter_dimension=0,
        tiled=True,
    )
    hidden = (jax.nn.silu(gate_up[:, :hidden_local]) * gate_up[:, hidden_local:]).astype(
        jnp.bfloat16
    )
    down_part = jnp.dot(
        lax.all_gather(hidden, "pool", axis=0, tiled=True),
        w_down,
        preferred_element_type=jnp.float32,
    )
    out_rows = (
        middle + lax.psum(down_part.astype(jnp.bfloat16), "tensor").astype(jnp.float32)
    ).astype(jnp.bfloat16)
    move_pages = mig_page[0]
    move_dest = mig_dest[0]
    move_slot = mig_slot[0]
    move_count = move_pages.shape[0]
    local_slots = key_value_pages.shape[0]
    dest_hot = (move_dest[:, None] == pool_iota[None, :]).astype(jnp.int32)
    move_rank = jnp.sum(jnp.cumsum(dest_hot, axis=0) * dest_hot, axis=1) - 1
    cap_iota = jnp.arange(MCAP, dtype=jnp.int32)
    move_hits = (move_dest[:, None, None] == pool_iota[None, :, None]) & (
        move_rank[:, None, None] == cap_iota[None, None, :]
    )
    move_iota = jnp.arange(move_count, dtype=jnp.int32)
    move_pick = jnp.sum(jnp.where(move_hits, move_iota[:, None, None], 0), axis=0)
    move_filled = jnp.any(move_hits, axis=0)
    send_pages = jnp.where(
        move_filled[:, :, None, None, None],
        key_value_pages[move_pages[move_pick]],
        jnp.zeros((), jnp.bfloat16),
    )
    send_slots = jnp.where(move_filled, move_slot[move_pick], local_slots)
    got_pages, got_slots = (
        lax.all_to_all(send_pages, "pool", split_axis=0, concat_axis=0, tiled=True),
        lax.all_to_all(send_slots, "pool", split_axis=0, concat_axis=0, tiled=True),
    )
    new_pool = key_value_pages.at[got_slots.reshape(-1)].set(
        got_pages.reshape(-1, page_len, kv_local, 2 * head_dim), mode="drop"
    )
    return (out_rows, new_pool)


def solution(mesh):
    return jax.shard_map(
        per_device,
        mesh=mesh,
        in_specs=(
            P(None, "pool"),
            P("pool"),
            P("pool", "tensor"),
            P("pool", None, "tensor", None),
            P("tensor", "pool"),
            P("pool"),
            P("pool", None, "tensor"),
            P("tensor", "pool"),
            P(),
            P(),
            P(),
            P("pool", None),
            P("pool", None),
            P("pool", None),
        ),
        out_specs=(P(None, "pool"), P("pool", None, "tensor", None)),
        check_vma=False,
    )
```

profile of v0, /device:TPU:0, one launch (start us, length us, event | category | flops | bytes accessed | tf_op | source)
XLA Modules:
  0.0 855.2 jit_solution(3642810041750591851)
XLA Ops:
  12.4 40.7 %psum.28 = f32[1024]{0:T(1024)S(1)} all-reduce(f32[1024]{0:T(1024)S(1)} %fusion.20), channel_id=1, replica_groups=mesh['pool'=16,'tensor'=8] {'pool'}, use_global_device_ids=true, to_apply=%region_5.6 | all-reduce | flops 1024 | bytes 8192 | tf_op jit(solution)/shard_map/psum | solution.py:55
  64.9 68.5 %reduce-scatter.3.cloned.1.call-done = f32[64,1280]{1,0:T(8,128)} async-done(((f32[1024,1280]{1,0:T(8,128)}), f32[64,1280]{1,0:T(8,128)}) %reduce-scatter.3.cloned.1.call-update) | async-done | bytes 327696 | tf_op jit(solution)/shard_map/reduce_scatter | solution.py:66
  142.2 8.8 %all-to-all-done.1 = bf16[16,8,1280]{2,1,0:T(8,128)(2,1)S(1)} async-done(((bf16[16,8,1280]{2,1,0:T(8,128)(2,1)}), bf16[16,8,1280]{2,1,0:T(8,128)(2,1)S(1)}, u32[]{:S(2)}, u32[]{:S(2)}) %all-to-all-start.1) | async-done | bytes 327712 | tf_op jit(solution)/shard_map/all_to_all | solution.py:99
  151.0 187.4 %while.10 = (s32[]{:T(128)}, bf16[16,8,1024]{2,1,0:T(8,128)(2,1)}, s32[16,8]{1,0:T(8,128)S(1)}, s32[1024]{0:T(1024)S(1)}, bf16[16,8,1280]{2,1,0:T(8,128)(2,1)S(1...) while((s32[]{:T(128)}, bf16[16,8,1024]{2,1,0:T(8,128)(2,1)}, ...), condition=%wide.region_10.11_spmd, body=%wide.region_7.10_spmd.sunk | while | flops 34262696 | bytes 13621417 | solution.py:142
  152.6 4.9 gather_fusion.1
  164.3 4.9 gather_fusion.1
  187.7 4.9 gather_fusion.1
  199.4 4.9 gather_fusion.1
  222.8 4.9 gather_fusion.1
  234.5 4.9 gather_fusion.1
  258.0 4.9 gather_fusion.1
  342.0 8.6 %all-to-all-done.2 = bf16[16,8,1024]{2,1,0:T(8,128)(2,1)S(1)} async-done(((bf16[16,8,1024]{2,1,0:T(8,128)(2,1)}), bf16[16,8,1024]{2,1,0:T(8,128)(2,1)S(1)}, u32[]{:S(2)}, u32[]{:S(2)}) %all-to-all-start.2) | async-done | bytes 262176 | tf_op jit(solution)/shard_map/all_to_all | solution.py:143
  352.4 42.5 %all-gather.3.cloned.1.call-done = bf16[1024,1024]{1,0:T(8,128)(2,1)} async-done(((bf16[64,1024]{1,0:T(8,128)(2,1)}), bf16[1024,1024]{1,0:T(8,128)(2,1)}) %all-gather.3.cloned.1.call-update) | async-done | bytes 2097168 | tf_op jit(solution)/shard_map/all_gather | solution.py:146
  399.7 7.8 copy.104
  407.5 57.1 %all-reduce.3.cloned.1.call-done = f32[1024,512]{1,0:T(8,128)} async-done(((f32[1024,512]{1,0:T(8,128)}), f32[1024,512]{1,0:T(8,128)}) %all-reduce.3.cloned.1.call-update) | async-done | bytes 2097168 | tf_op jit(solution)/shard_map/psum | solution.py:150
  466.6 40.5 %psum.30 = f32[1024]{0:T(1024)S(1)} all-reduce(f32[1024]{0:T(1024)S(1)} %multiply_reduce_fusion), channel_id=1, replica_groups=mesh['pool'=16,'tensor'=8] {'pool'}, use_global_device_ids=true, to_apply=%region_13.14 | all-reduce | flops 1024 | bytes 8192 | tf_op jit(solution)/shard_map/psum | solution.py:151
  507.1 16.4 %fusion.23 = f32[1024,7168]{1,0:T(8,128)} fusion(bf16[512,7168]{1,0:T(8,128)(2,1)} %bitcast.147, f32[512]{0:T(512)S(1)} %convert_element_type.70, f32[1024]{0:T(1024)S(1)} %add_rsqrt_fusion, f32[1024,512]{1,0:T(8,128)} %all-reduce.3.cloned.1.call-done, bf16[1024,512]{1,0:T(8,128)(2,1)S(1)} %copy-done.5), kind=kOutput, calls=%fused_computation.59 | convolution fusion | flops 7518814208 | bytes 39852032 | tf_op jit(solution)/shard_map/dot_general | solution.py:160
  523.6 168.2 %reduce-scatter.5.cloned.1.call-done = f32[64,7168]{1,0:T(8,128)} async-done(((f32[1024,7168]{1,0:T(8,128)}), f32[64,7168]{1,0:T(8,128)}) %reduce-scatter.5.cloned.1.call-update) | async-done | bytes 1835024 | tf_op jit(solution)/shard_map/reduce_scatter | solution.py:159
  696.5 5.3 all-to-all-start.3
  710.6 7.3 all-to-all-start.4
  718.0 55.6 %all-gather.5.cloned.1.call-done = bf16[1024,3584]{1,0:T(8,128)(2,1)} async-done(((bf16[64,3584]{1,0:T(8,128)(2,1)}), bf16[1024,3584]{1,0:T(8,128)(2,1)}) %all-gather.5.cloned.1.call-update) | async-done | bytes 7340048 | tf_op jit(solution)/shard_map/all_gather | solution.py:169
  773.6 9.0 %convolution_convert_fusion = bf16[1024,512]{1,0:T(8,128)(2,1)} fusion(bf16[1024,3584]{1,0:T(8,128)(2,1)} %all-gather.5.cloned.1.call-done, bf16[3584,512]{1,0:T(8,128)(2,1)} %param.23), kind=kOutput, calls=%fused_computation.58 | convolution fusion | flops 3758620672 | bytes 12058624 | tf_op jit(solution)/shard_map/dot_general | solution.py:168
  784.1 6.0 scatter_fusion
  790.1 55.0 %all-reduce.5.cloned.1.call-done = bf16[1024,512]{1,0:T(8,128)(2,1)} async-done(((bf16[1024,512]{1,0:T(8,128)(2,1)}), bf16[1024,512]{1,0:T(8,128)(2,1)}) %all-reduce.5.cloned.1.call-update) | async-done | bytes 1048592 | tf_op jit(solution)/shard_map/psum | solution.py:174
  (448 shorter events, 208.1 us)
Async XLA Ops:
  7.2 46.0 %copy-start = (bf16[512,1280]{1,0:T(8,128)(2,1)S(1)}, bf16[512,1280]{1,0:T(8,128)(2,1)}, u32[]{:S(2)}) copy-start(bf16[512,1280]{1,0:T(8,128)(2,1)} %param.18) | copy-start | bytes 3932164
  7.2 4.9 copy-start.5
  7.2 4.9 copy-start.9
  7.2 126.2 %reduce-scatter.3.cloned.1.call-start = ((), (), s32[]{:S(2)}) async-start(), calls=%async_computation.7 | async-start | bytes 5570560 | tf_op jit(solution)/shard_map/reduce_scatter | solution.py:66
  57.0 0.7 copy-start.7
  57.0 7.6 copy-start.4
  60.9 76.2 %all-to-all-start = ((s32[16,1,8]{2,1,0:T(1,128)}), s32[16,1,8]{2,1,0:T(1,128)S(1)}, u32[]{:S(2)}, u32[]{:S(2)}) async-start(s32[16,1,8]{2,1,0:T(1,128)} %bitcast.37), calls=%async_computation | async-start | bytes 16384 | tf_op jit(solution)/shard_map/all_to_all | solution.py:100
  135.3 6.6 copy-start.6
  137.1 13.9 %all-to-all-start.1 = ((bf16[16,8,1280]{2,1,0:T(8,128)(2,1)}), bf16[16,8,1280]{2,1,0:T(8,128)(2,1)S(1)}, u32[]{:S(2)}, u32[]{:S(2)}) async-start(bf16[16,8,1280]{2,1,0:T(8,128)(2,1)} %fusion.33), calls=%async_computation.2 | async-start | bytes 655360 | tf_op jit(solution)/shard_map/all_to_all | solution.py:99
  151.0 243.8 %copy-start.11 = (bf16[1024,512]{1,0:T(8,128)(2,1)S(1)}, bf16[1024,512]{1,0:T(8,128)(2,1)}, u32[]{:S(2)}) copy-start(bf16[1024,512]{1,0:T(8,128)(2,1)} %param.20) | copy-start | bytes 3145732
  338.4 12.2 %all-to-all-start.2 = ((bf16[16,8,1024]{2,1,0:T(8,128)(2,1)}), bf16[16,8,1024]{2,1,0:T(8,128)(2,1)S(1)}, u32[]{:S(2)}, u32[]{:S(2)}) async-start(bf16[16,8,1024]{2,1,0:T(8,128)(2,1)} %get-tuple-element.39), calls=%async_computation.3 | async-start | bytes 524288 | tf_op jit(solution)/shard_map/all_to_all | solution.py:143
  341.9 52.9 %all-gather.3.cloned.1.call-start = ((), (), s32[]{:S(2)}) async-start(), calls=%async_computation.8 | async-start | bytes 2228224 | tf_op jit(solution)/shard_map/all_gather | solution.py:146
  352.3 112.3 %all-reduce.3.cloned.1.call-start = ((), (), s32[]{:S(2)}) async-start(), calls=%async_computation.9 | async-start | bytes 4194304 | tf_op jit(solution)/shard_map/psum | solution.py:150
  399.0 0.7 copy-start.10
  399.0 292.7 %reduce-scatter.5.cloned.1.call-start = ((), (), s32[]{:S(2)}) async-start(), calls=%async_computation.10 | async-start | bytes 31195136 | tf_op jit(solution)/shard_map/reduce_scatter | solution.py:159
  523.5 170.7 %copy-start.8 = (s32[1,16]{1,0:T(1,128)S(1)}, s32[1,16]{1,0:T(1,128)}, u32[]{:S(2)}) copy-start(s32[1,16]{1,0:T(1,128)} %param.28) | copy-start | bytes 196
  523.5 171.3 %copy-start.2 = (s32[1,16]{1,0:T(1,128)S(1)}, s32[1,16]{1,0:T(1,128)}, u32[]{:S(2)}) copy-start(s32[1,16]{1,0:T(1,128)} %param.29) | copy-start | bytes 196
  523.5 250.1 %all-gather.5.cloned.1.call-start = ((), (), s32[]{:S(2)}) async-start(), calls=%async_computation.11 | async-start | bytes 7798784 | tf_op jit(solution)/shard_map/all_gather | solution.py:169
  695.6 6.4 copy-start.3
  696.5 14.1 %all-to-all-start.3 = ((s32[16,1,2]{2,1,0:T(1,128)}), s32[16,1,2]{2,1,0:T(1,128)S(1)}, u32[]{:S(2)}, u32[]{:S(2)}) async-start(s32[16,1,2]{2,1,0:T(1,128)} %copy.91), calls=%async_computation.5 | async-start | bytes 16384 | tf_op jit(solution)/shard_map/all_to_all | solution.py:198
  710.6 73.5 %all-to-all-start.4 = ((bf16[16,2,128,1,256]{4,2,1,3,0:T(8,128)(2,1)}), bf16[16,2,128,1,256]{4,2,1,3,0:T(8,128)(2,1)}, u32[]{:S(2)}, u32[]{:S(2)}) async-start(bf16[16,2,128,1,256]{4,2,1,3,0:T(8,128)(2,1)} %broadcast_select_fusion), calls=%async_computation.6 | async-start | bytes 4194304 | tf_op jit(solution)/shard_map/all_to_all | solution.py:197
  718.0 127.1 %all-reduce.5.cloned.1.call-start = ((), (), s32[]{:S(2)}) async-start(), calls=%async_computation.12 | async-start | bytes 2097152 | tf_op jit(solution)/shard_map/psum | solution.py:174
  784.1 64.3 %copy-start.1 = (bf16[512,1280]{1,0:T(8,128)(2,1)S(1)}, bf16[512,1280]{1,0:T(8,128)(2,1)}, u32[]{:S(2)}) copy-start(bf16[512,1280]{1,0:T(8,128)(2,1)} %param.18) | copy-start | bytes 3932164
Sparse Core Ops, SparseCore 0:
  57.2 76.1 reduce-scatter.2
  352.4 42.3 all-gather.2
  399.2 65.4 all-reduce.2
  523.6 168.0 reduce-scatter.4
  694.4 79.2 all-gather.4
  782.8 62.1 all-reduce.4
where the time goes:
time: 858 us; the launch traced here: 855 us
  waiting for transfers between devices  464 us (54%)
  local copies, waits for them, and re-layouts  142 us (17%)
  matrix products  105 us (12%)
  blocking collectives  81.2 us (9%)
  starting transfers between devices  24.8 us (3%)
  other arithmetic  22.7 us (3%)
  between operations  14.5 us (2%)
    reduce_scatter x1, waiting for transfers between devices, per_device(): lax.psum_scatter(jnp.dot(ffn_in, joined_weight, preferred_element_type=jn...  168 us
    gather x16, local copies, waits for them, and re-layouts, one_block(): key_value_pages[table]  78.9 us
    reduce_scatter x1, waiting for transfers between devices, per_device(): lax.psum_scatter(jnp.dot(normed_input, query_key_value_weight, preferred_...  68.5 us
    psum x1, waiting for transfers between devices, per_device(): middle = residual + lax.psum(partial_value, 'tensor')  57.1 us
    all_gather x1, waiting for transfers between devices, per_device(): lax.all_gather(hidden, 'pool', axis=0, tiled=True)  55.6 us
    psum x1, waiting for transfers between devices, per_device(): lax.psum(down_part.astype(jnp.bfloat16), 'tensor').astype(jnp.float32)  55 us
    all_gather x1, waiting for transfers between devices, per_device(): lax.all_gather(my_rows, 'pool', axis=0, tiled=True)  42.5 us
    psum x1, blocking collectives, per_device(): squares = lax.psum(jnp.sum(residual * residual, axis=1), 'pool')  40.7 us
  transfers between devices with their start and end apart: 11, of which 8 were waited for; matrix products, arithmetic and copies ran while one was open for 5% of the time, Pallas kernels for 0%

commit v1 on v0

--- a/solution.py
+++ b/solution.py
@@ -6,6 +6,22 @@
 
 MCAP = 2
 epsilon = 1e-05
+
+
+def collect(x, axis, dim):
+    ways, here, hop = (lax.axis_size(axis), lax.axis_index(axis), x.shape[dim])
+    dims = [n * ways if d == dim else n for d, n in enumerate(x.shape)]
+    full = lax.dynamic_update_slice_in_dim(jnp.zeros(dims, x.dtype), x, here * hop, axis=dim)
+    going_up = going_down = x
+    for far in range(1, ways // 2 + 1):
+        going_up = lax.ppermute(going_up, axis, [(d, (d + 1) % ways) for d in range(ways)])
+        full = lax.dynamic_update_slice_in_dim(full, going_up, (here - far) % ways * hop, axis=dim)
+        if 2 * far < ways:
+            going_down = lax.ppermute(going_down, axis, [(d, (d - 1) % ways) for d in range(ways)])
+            full = lax.dynamic_update_slice_in_dim(
+                full, going_down, (here + far) % ways * hop, axis=dim
+            )
+    return full
 
 
 def rotate_halves(vectors, token_positions):
@@ -165,11 +181,7 @@
     hidden = (jax.nn.silu(gate_up[:, :hidden_local]) * gate_up[:, hidden_local:]).astype(
         jnp.bfloat16
     )
-    down_part = jnp.dot(
-        lax.all_gather(hidden, "pool", axis=0, tiled=True),
-        w_down,
-        preferred_element_type=jnp.float32,
-    )
+    down_part = jnp.dot(collect(hidden, "pool", 0), w_down, preferred_element_type=jnp.float32)
     out_rows = (
         middle + lax.psum(down_part.astype(jnp.bfloat16), "tensor").astype(jnp.float32)
     ).astype(jnp.bfloat16)

time: 858 us -> 899 us (1.048)
  starting transfers between devices: 24.8 us -> 60.1 us
  local copies, waits for them, and re-layouts: 142 us -> 157 us
    ppermute x0 -> x15, waiting for transfers between devices: none -> 57.2 us  [the longest x8 57.2 us: collect(): lax.ppermute(going_up, axis, [(d, (d + 1) % ways) for d in range(ways)])]
    all_gather x1 -> x0, waiting for transfers between devices: 55.6 us -> none  [per_device(): lax.all_gather(hidden, 'pool', axis=0, tiled=True)]
    ppermute x0 -> x15, starting transfers between devices: none -> 37.5 us  [the longest x7 36.2 us: collect(): lax.ppermute(going_down, axis, [(d, (d - 1) % ways) for d in range(ways)])]
    dynamic_update_slice x0 -> x15, local copies, waits for them, and re-layouts: none -> 12.2 us  [the longest x8 6.52 us: collect(): lax.dynamic_update_slice_in_dim(full, going_up, (here - far) % ways * hop...]
  transfers between devices with their start and end apart: 11 -> 25, of which waited for: 8 -> 15; matrix products, arithmetic and copies ran while one was open for 5% -> 7% of each run, Pallas kernels for 0% -> 0%
where the time goes in v1:
time: 899 us; the launch traced here: 896 us
  waiting for transfers between devices  456 us (51%)
  local copies, waits for them, and re-layouts  157 us (17%)
  matrix products  105 us (12%)
  blocking collectives  81.2 us (9%)
  starting transfers between devices  60.1 us (7%)
  other arithmetic  21.2 us (2%)
  between operations  14.3 us (2%)
    reduce_scatter x1, waiting for transfers between devices, per_device(): lax.psum_scatter(jnp.dot(ffn_in, joined_weight, preferred_element_type=jn...  161 us
    gather x16, local copies, waits for them, and re-layouts, one_block(): key_value_pages[table]  79.1 us
    reduce_scatter x1, waiting for transfers between devices, per_device(): lax.psum_scatter(jnp.dot(normed_input, query_key_value_weight, preferred_...  68.6 us
    psum x1, waiting for transfers between devices, per_device(): middle = residual + lax.psum(partial_value, 'tensor')  57.7 us
    ppermute x8, waiting for transfers between devices, collect(): lax.ppermute(going_up, axis, [(d, (d + 1) % ways) for d in range(ways)])  57.2 us
    psum x1, waiting for transfers between devices, per_device(): lax.psum(down_part.astype(jnp.bfloat16), 'tensor').astype(jnp.float32)  52.1 us
    all_gather x1, waiting for transfers between devices, per_device(): lax.all_gather(my_rows, 'pool', axis=0, tiled=True)  42.5 us
    psum x1, blocking collectives, per_device(): squares = lax.psum(jnp.sum(residual * residual, axis=1), 'pool')  40.7 us
  transfers between devices with their start and end apart: 25, of which 15 were waited for; matrix products, arithmetic and copies ran while one was open for 7% of the time, Pallas kernels for 0%

profile of v1, /device:TPU:0, one launch (start us, length us, event | category | flops | bytes accessed | tf_op | source)
XLA Modules:
  0.0 896.5 jit_solution(8981586879267934674)
XLA Ops:
  12.4 40.7 %psum.28 = f32[1024]{0:T(1024)S(1)} all-reduce(f32[1024]{0:T(1024)S(1)} %fusion.20), channel_id=1, replica_groups=mesh['pool'=16,'tensor'=8] {'pool'}, use_global_device_ids=true, to_apply=%region_5.6 | all-reduce | flops 1024 | bytes 8192 | tf_op jit(solution)/shard_map/psum | solution.py:71
  64.9 68.6 %reduce-scatter.3.cloned.1.call-done = f32[64,1280]{1,0:T(8,128)} async-done(((f32[1024,1280]{1,0:T(8,128)}), f32[64,1280]{1,0:T(8,128)}) %reduce-scatter.3.cloned.1.call-update) | async-done | bytes 327696 | tf_op jit(solution)/shard_map/reduce_scatter | solution.py:82
  142.2 8.8 all-to-all-done.1
  151.0 187.6 %while.10 = (s32[]{:T(128)}, bf16[16,8,1024]{2,1,0:T(8,128)(2,1)}, s32[16,8]{1,0:T(8,128)S(1)}, s32[1024]{0:T(1024)S(1)}, bf16[16,8,1280]{2,1,0:T(8,128)(2,1)S(1...) while((s32[]{:T(128)}, bf16[16,8,1024]{2,1,0:T(8,128)(2,1)}, ...), condition=%wide.region_10.11_spmd, body=%wide.region_7.10_spmd.sunk | while | flops 34262696 | bytes 13621917 | solution.py:158
  342.3 8.6 all-to-all-done.2
  352.7 42.5 %all-gather.2.cloned.1.call-done = bf16[1024,1024]{1,0:T(8,128)(2,1)} async-done(((bf16[64,1024]{1,0:T(8,128)(2,1)}), bf16[1024,1024]{1,0:T(8,128)(2,1)}) %all-gather.2.cloned.1.call-update) | async-done | bytes 2097168 | tf_op jit(solution)/shard_map/all_gather | solution.py:162
  399.4 7.8 copy.104
  407.2 57.7 %all-reduce.3.cloned.1.call-done = f32[1024,512]{1,0:T(8,128)} async-done(((f32[1024,512]{1,0:T(8,128)}), f32[1024,512]{1,0:T(8,128)}) %all-reduce.3.cloned.1.call-update) | async-done | bytes 2097168 | tf_op jit(solution)/shard_map/psum | solution.py:166
  466.8 40.5 %psum.30 = f32[1024]{0:T(1024)S(1)} all-reduce(f32[1024]{0:T(1024)S(1)} %multiply_reduce_fusion), channel_id=1, replica_groups=mesh['pool'=16,'tensor'=8] {'pool'}, use_global_device_ids=true, to_apply=%region_13.14 | all-reduce | flops 1024 | bytes 8192 | tf_op jit(solution)/shard_map/psum | solution.py:167
  507.3 16.4 %fusion.23 = f32[1024,7168]{1,0:T(8,128)} fusion(bf16[512,7168]{1,0:T(8,128)(2,1)} %bitcast.146, f32[512]{0:T(512)S(1)} %convert_element_type.70, f32[1024]{0:T(1024)S(1)} %add_rsqrt_fusion, f32[1024,512]{1,0:T(8,128)} %all-reduce.3.cloned.1.call-done, bf16[1024,512]{1,0:T(8,128)(2,1)S(1)} %copy-done.5), kind=kOutput, calls=%fused_computation.59 | convolution fusion | flops 7518814208 | bytes 39852032 | tf_op jit(solution)/shard_map/dot_general | solution.py:176
  531.1 161.0 %reduce-scatter.5.cloned.1.call-done = f32[64,7168]{1,0:T(8,128)} async-done(((f32[1024,7168]{1,0:T(8,128)}), f32[64,7168]{1,0:T(8,128)}) %reduce-scatter.5.cloned.1.call-update) | async-done | bytes 1835024 | tf_op jit(solution)/shard_map/reduce_scatter | solution.py:175
  712.2 5.3 collective-permute-start.3
  719.2 7.8 collective-permute-done.2
  727.0 5.3 collective-permute-start.5
  733.9 6.9 collective-permute-done.4
  740.8 5.3 collective-permute-start.7
  747.8 6.0 collective-permute-done.6
  777.5 5.5 collective-permute-start.13
  784.6 5.7 collective-permute-done.12
  791.9 6.8 all-to-all-start.4
  799.0 18.5 %collective-permute-done.14 = bf16[64,3584]{1,0:T(8,128)(2,1)S(1)} collective-permute-done((bf16[64,3584]{1,0:T(8,128)(2,1)S(1)}, bf16[64,3584]{1,0:T(8,128)(2,1)S(1)}, u32[]{:S(2)}, u32[]{:S(2)}) %collective-permute-start.14) | collective-permute-done | bytes 458784 | tf_op jit(solution)/shard_map/ppermute | solution.py:17
  818.3 9.0 %convolution_convert_fusion = bf16[1024,512]{1,0:T(8,128)(2,1)} fusion(bf16[1024,3584]{1,0:T(8,128)(2,1)} %constant_dynamic-update-slice_fusion.1, bf16[3584,512]{1,0:T(8,128)(2,1)} %param.23), kind=kOutput, calls=%fused_computation.58 | convolution fusion | flops 3758620672 | bytes 12058624 | tf_op jit(solution)/shard_map/dot_general | solution.py:184
  828.6 6.0 scatter_fusion
  834.6 52.1 %all-reduce.5.cloned.1.call-done = bf16[1024,512]{1,0:T(8,128)(2,1)} async-done(((bf16[1024,512]{1,0:T(8,128)(2,1)}), bf16[1024,512]{1,0:T(8,128)(2,1)}) %all-reduce.5.cloned.1.call-update) | async-done | bytes 1048592 | tf_op jit(solution)/shard_map/psum | solution.py:186
  (493 shorter events, 288.7 us)
Async XLA Ops:
  7.2 126.3 %reduce-scatter.3.cloned.1.call-start = ((), (), s32[]{:S(2)}) async-start(), calls=%async_computation.7 | async-start | bytes 5570560 | tf_op jit(solution)/shard_map/reduce_scatter | solution.py:82
  60.9 76.2 %all-to-all-start = ((s32[16,1,8]{2,1,0:T(1,128)}), s32[16,1,8]{2,1,0:T(1,128)S(1)}, u32[]{:S(2)}, u32[]{:S(2)}) async-start(s32[16,1,8]{2,1,0:T(1,128)} %bitcast.37), calls=%async_computation | async-start | bytes 16384 | tf_op jit(solution)/shard_map/all_to_all | solution.py:116
  137.1 13.9 %all-to-all-start.1 = ((bf16[16,8,1280]{2,1,0:T(8,128)(2,1)}), bf16[16,8,1280]{2,1,0:T(8,128)(2,1)S(1)}, u32[]{:S(2)}, u32[]{:S(2)}) async-start(bf16[16,8,1280]{2,1,0:T(8,128)(2,1)} %fusion.33), calls=%async_computation.2 | async-start | bytes 655360 | tf_op jit(solution)/shard_map/all_to_all | solution.py:115
  338.7 12.2 %all-to-all-start.2 = ((bf16[16,8,1024]{2,1,0:T(8,128)(2,1)}), bf16[16,8,1024]{2,1,0:T(8,128)(2,1)S(1)}, u32[]{:S(2)}, u32[]{:S(2)}) async-start(bf16[16,8,1024]{2,1,0:T(8,128)(2,1)} %get-tuple-element.39), calls=%async_computation.3 | async-start | bytes 524288 | tf_op jit(solution)/shard_map/all_to_all | solution.py:159
  342.2 52.9 %all-gather.2.cloned.1.call-start = ((), (), s32[]{:S(2)}) async-start(), calls=%async_computation.8 | async-start | bytes 2228224 | tf_op jit(solution)/shard_map/all_gather | solution.py:162
  352.6 112.3 %all-reduce.3.cloned.1.call-start = ((), (), s32[]{:S(2)}) async-start(), calls=%async_computation.9 | async-start | bytes 4194304 | tf_op jit(solution)/shard_map/psum | solution.py:166
  399.3 292.8 %reduce-scatter.5.cloned.1.call-start = ((), (), s32[]{:S(2)}) async-start(), calls=%async_computation.10 | async-start | bytes 31195136 | tf_op jit(solution)/shard_map/reduce_scatter | solution.py:175
  526.7 265.2 %all-to-all-start.3 = ((s32[16,1,2]{2,1,0:T(1,128)}), s32[16,1,2]{2,1,0:T(1,128)S(1)}, u32[]{:S(2)}, u32[]{:S(2)}) async-start(s32[16,1,2]{2,1,0:T(1,128)} %copy.91), calls=%async_computation.5 | async-start | bytes 16384 | tf_op jit(solution)/shard_map/all_to_all | solution.py:210
  696.6 15.6 %collective-permute-start = (bf16[64,3584]{1,0:T(8,128)(2,1)S(1)}, bf16[64,3584]{1,0:T(8,128)(2,1)S(1)}, u32[]{:S(2)}, u32[]{:S(2)}) collective-permute-start(bf16[64,3584]{1,0:T(8,128)(2,1)S(1)} %get-tuple-element.90), channel_id=1, source_target_pairs={{0,8},{8,16},{16,24},{24,32},{32,40},{40,48},{48,56},{56,64},{64,7... | collective-permute-start | bytes 1376264 | tf_op jit(solution)/shard_map/ppermute | solution.py:17
  697.9 14.3 %collective-permute-start.1 = (bf16[64,3584]{1,0:T(8,128)(2,1)S(1)}, bf16[64,3584]{1,0:T(8,128)(2,1)S(1)}, u32[]{:S(2)}, u32[]{:S(2)}) collective-permute-start(bf16[64,3584]{1,0:T(8,128)(2,1)S(1)} %get-tuple-element.90), channel_id=1, source_target_pairs={{0,120},{8,0},{16,8},{24,16},{32,24},{40,32},{48,40},{56,48},{64,5... | collective-permute-start | bytes 1376264 | tf_op jit(solution)/shard_map/ppermute | solution.py:20
  712.2 14.8 %collective-permute-start.2 = (bf16[64,3584]{1,0:T(8,128)(2,1)S(1)}, bf16[64,3584]{1,0:T(8,128)(2,1)S(1)}, u32[]{:S(2)}, u32[]{:S(2)}) collective-permute-start(bf16[64,3584]{1,0:T(8,128)(2,1)S(1)} %collective-permute-done), channel_id=1, source_target_pairs={{0,8},{8,16},{16,24},{24,32},{32,40},{40,48},{48,56},{56,64},{64,7... | collective-permute-start | bytes 1376264 | tf_op jit(solution)/shard_map/ppermute | solution.py:17
  712.2 14.8 %collective-permute-start.3 = (bf16[64,3584]{1,0:T(8,128)(2,1)S(1)}, bf16[64,3584]{1,0:T(8,128)(2,1)S(1)}, u32[]{:S(2)}, u32[]{:S(2)}) collective-permute-start(bf16[64,3584]{1,0:T(8,128)(2,1)S(1)} %collective-permute-done.1), channel_id=1, source_target_pairs={{0,120},{8,0},{16,8},{24,16},{32,24},{40,32},{48,40},{56,48},{64,5... | collective-permute-start | bytes 1376264 | tf_op jit(solution)/shard_map/ppermute | solution.py:20
  727.0 13.8 %collective-permute-start.4 = (bf16[64,3584]{1,0:T(8,128)(2,1)S(1)}, bf16[64,3584]{1,0:T(8,128)(2,1)S(1)}, u32[]{:S(2)}, u32[]{:S(2)}) collective-permute-start(bf16[64,3584]{1,0:T(8,128)(2,1)S(1)} %collective-permute-done.2), channel_id=1, source_target_pairs={{0,8},{8,16},{16,24},{24,32},{32,40},{40,48},{48,56},{56,64},{64,7... | collective-permute-start | bytes 1376264 | tf_op jit(solution)/shard_map/ppermute | solution.py:17
  727.0 13.8 %collective-permute-start.5 = (bf16[64,3584]{1,0:T(8,128)(2,1)S(1)}, bf16[64,3584]{1,0:T(8,128)(2,1)S(1)}, u32[]{:S(2)}, u32[]{:S(2)}) collective-permute-start(bf16[64,3584]{1,0:T(8,128)(2,1)S(1)} %collective-permute-done.3), channel_id=1, source_target_pairs={{0,120},{8,0},{16,8},{24,16},{32,24},{40,32},{48,40},{56,48},{64,5... | collective-permute-start | bytes 1376264 | tf_op jit(solution)/shard_map/ppermute | solution.py:20
  740.8 12.9 %collective-permute-start.6 = (bf16[64,3584]{1,0:T(8,128)(2,1)S(1)}, bf16[64,3584]{1,0:T(8,128)(2,1)S(1)}, u32[]{:S(2)}, u32[]{:S(2)}) collective-permute-start(bf16[64,3584]{1,0:T(8,128)(2,1)S(1)} %collective-permute-done.4), channel_id=1, source_target_pairs={{0,8},{8,16},{16,24},{24,32},{32,40},{40,48},{48,56},{56,64},{64,7... | collective-permute-start | bytes 1376264 | tf_op jit(solution)/shard_map/ppermute | solution.py:17
  740.8 12.9 %collective-permute-start.7 = (bf16[64,3584]{1,0:T(8,128)(2,1)S(1)}, bf16[64,3584]{1,0:T(8,128)(2,1)S(1)}, u32[]{:S(2)}, u32[]{:S(2)}) collective-permute-start(bf16[64,3584]{1,0:T(8,128)(2,1)S(1)} %collective-permute-done.5), channel_id=1, source_target_pairs={{0,120},{8,0},{16,8},{24,16},{32,24},{40,32},{48,40},{56,48},{64,5... | collective-permute-start | bytes 1376264 | tf_op jit(solution)/shard_map/ppermute | solution.py:20
  753.7 12.0 %collective-permute-start.8 = (bf16[64,3584]{1,0:T(8,128)(2,1)S(1)}, bf16[64,3584]{1,0:T(8,128)(2,1)S(1)}, u32[]{:S(2)}, u32[]{:S(2)}) collective-permute-start(bf16[64,3584]{1,0:T(8,128)(2,1)S(1)} %collective-permute-done.6), channel_id=1, source_target_pairs={{0,8},{8,16},{16,24},{24,32},{32,40},{40,48},{48,56},{56,64},{64,7... | collective-permute-start | bytes 1376264 | tf_op jit(solution)/shard_map/ppermute | solution.py:17
  753.7 12.0 %collective-permute-start.9 = (bf16[64,3584]{1,0:T(8,128)(2,1)S(1)}, bf16[64,3584]{1,0:T(8,128)(2,1)S(1)}, u32[]{:S(2)}, u32[]{:S(2)}) collective-permute-start(bf16[64,3584]{1,0:T(8,128)(2,1)S(1)} %collective-permute-done.7), channel_id=1, source_target_pairs={{0,120},{8,0},{16,8},{24,16},{32,24},{40,32},{48,40},{56,48},{64,5... | collective-permute-start | bytes 1376264 | tf_op jit(solution)/shard_map/ppermute | solution.py:20
  765.7 11.8 %collective-permute-start.10 = (bf16[64,3584]{1,0:T(8,128)(2,1)S(1)}, bf16[64,3584]{1,0:T(8,128)(2,1)S(1)}, u32[]{:S(2)}, u32[]{:S(2)}) collective-permute-start(bf16[64,3584]{1,0:T(8,128)(2,1)S(1)} %collective-permute-done.8), channel_id=1, source_target_pairs={{0,8},{8,16},{16,24},{24,32},{32,40},{40,48},{48,56},{56,64},{64,7... | collective-permute-start | bytes 1376264 | tf_op jit(solution)/shard_map/ppermute | solution.py:17
  777.5 12.8 %collective-permute-start.12 = (bf16[64,3584]{1,0:T(8,128)(2,1)S(1)}, bf16[64,3584]{1,0:T(8,128)(2,1)S(1)}, u32[]{:S(2)}, u32[]{:S(2)}) collective-permute-start(bf16[64,3584]{1,0:T(8,128)(2,1)S(1)} %collective-permute-done.10), channel_id=1, source_target_pairs={{0,8},{8,16},{16,24},{24,32},{32,40},{40,48},{48,56},{56,64},{64,7... | collective-permute-start | bytes 1376264 | tf_op jit(solution)/shard_map/ppermute | solution.py:17
  777.5 13.6 %collective-permute-start.13 = (bf16[64,3584]{1,0:T(8,128)(2,1)S(1)}, bf16[64,3584]{1,0:T(8,128)(2,1)S(1)}, u32[]{:S(2)}, u32[]{:S(2)}) collective-permute-start(bf16[64,3584]{1,0:T(8,128)(2,1)S(1)} %collective-permute-done.11), channel_id=1, source_target_pairs={{0,120},{8,0},{16,8},{24,16},{32,24},{40,32},{48,40},{56,48},{64,5... | collective-permute-start | bytes 1376264 | tf_op jit(solution)/shard_map/ppermute | solution.py:20
  790.3 27.2 %collective-permute-start.14 = (bf16[64,3584]{1,0:T(8,128)(2,1)S(1)}, bf16[64,3584]{1,0:T(8,128)(2,1)S(1)}, u32[]{:S(2)}, u32[]{:S(2)}) collective-permute-start(bf16[64,3584]{1,0:T(8,128)(2,1)S(1)} %collective-permute-done.12), channel_id=1, source_target_pairs={{0,8},{8,16},{16,24},{24,32},{32,40},{40,48},{48,56},{56,64},{64,7... | collective-permute-start | bytes 1376264 | tf_op jit(solution)/shard_map/ppermute | solution.py:17
  791.9 36.7 %all-to-all-start.4 = ((bf16[16,2,128,1,256]{4,2,1,3,0:T(8,128)(2,1)}), bf16[16,2,128,1,256]{4,2,1,3,0:T(8,128)(2,1)}, u32[]{:S(2)}, u32[]{:S(2)}) async-start(bf16[16,2,128,1,256]{4,2,1,3,0:T(8,128)(2,1)} %broadcast_select_fusion), calls=%async_computation.6 | async-start | bytes 4194304 | tf_op jit(solution)/shard_map/all_to_all | solution.py:209
  798.7 87.9 %all-reduce.5.cloned.1.call-start = ((), (), s32[]{:S(2)}) async-start(), calls=%async_computation.11 | async-start | bytes 2097152 | tf_op jit(solution)/shard_map/psum | solution.py:186
  (14 other events, 523.3 us)
Sparse Core Ops, SparseCore 0:
  57.2 76.2 reduce-scatter.2
  352.7 42.3 all-gather.1
  399.5 65.3 all-reduce.2
  523.9 168.1 reduce-scatter.4
  827.5 59.0 all-reduce.4
